TPU v7x, 32 devices: a whole 2x2x4 slice. The times are simulated.
32 devices in a mesh: dp: 8 (over y, x, core), expert: 4 (over z).
Axes of the slice: x: 2, y: 2, z: 4, core: 2. Of those that a mesh axis runs over, the one named last changes fastest.
Arguments:
- tokens: bfloat16 [4096, 4096], P(('dp', 'expert')), may hold values from -6 to 6
- probs: bfloat16 [4096, 1], P(('dp', 'expert')), may hold values from 0.19921875 to 1
- routes: int32 [4096, 1], P(('dp', 'expert')), may hold values from 0 to 3; in each aligned block of 128 rows (0 to 127, 128 to 255, ...) at most 34 rows name the same one
- w_gate: bfloat16 [4, 4096, 1024], P('expert', 'dp'), may hold values from -0.09375 to 0.09375
- w_up: bfloat16 [4, 4096, 1024], P('expert', 'dp'), may hold values from -0.09375 to 0.09375
- w_down: bfloat16 [4, 1024, 4096], P('expert', None, 'dp'), may hold values from -0.1875 to 0.1875
- cotangent: bfloat16 [4096, 4096], P(('dp', 'expert')), may hold values from -6 to 6
Outputs:
- mixed: bfloat16 [4096, 4096], P(('dp', 'expert'))
- input_grad: bfloat16 [4096, 4096], P(('dp', 'expert'))
- grad_gate: bfloat16 [4, 4096, 1024], P('expert', 'dp')
- grad_up: bfloat16 [4, 4096, 1024], P('expert', 'dp')
- grad_down: bfloat16 [4, 1024, 4096], P('expert', None, 'dp')
Inputs may be any that keep to these rules, and one draw needn't show every extreme that they name: `routes`: each row names exactly one expert. Among the 128 rows of one device (aligned blocks), no expert is named more than 34 times, a bound that some block reaches.
All inputs are finite; a program needn't handle non-finite values.
Results may differ from a plain program's by a relative error of at most 0.025.
Values may be sent and summed in bfloat16 or wider, within the bound.
A program may use at most 128 MiB of HBM per device.

v0:
```python
import jax
import jax.numpy as jnp
from jax import lax
from jax.sharding import PartitionSpec as P


def slot_table(routes, experts_all, capacity):
    flat = routes.reshape(-1)
    hits = (flat[:, None] == jnp.arange(experts_all, dtype=jnp.int32)[None, :]).astype(jnp.int32)
    before = jnp.cumsum(hits, axis=0) - hits
    place = jnp.sum(before * hits, axis=1)
    target = flat * capacity + place
    table = jnp.arange(experts_all * capacity, dtype=jnp.int32)[:, None] == target[None, :]
    return table.astype(jnp.bfloat16)


def spread_rows(table, values, slices):
    shaped = values.reshape(values.shape[0], slices, values.shape[1] // slices)
    return jnp.einsum("st,tnk->nsk", table, shaped, preferred_element_type=jnp.float32).astype(
        jnp.bfloat16
    )


def to_rows(received, local_count):
    sources, slots, width = received.shape
    shaped = received.reshape(sources, local_count, slots // local_count, width)
    shaped = jnp.swapaxes(shaped, 1, 2)
    return shaped.reshape(sources * (slots // local_count), local_count, width)


def to_sources(rowwise, capacity):
    total, local_count, width = rowwise.shape
    shaped = rowwise.reshape(total // capacity, capacity, local_count, width)
    shaped = jnp.swapaxes(shaped, 1, 2)
    return shaped.reshape(total // capacity, local_count * capacity, width)


def collect(table, back, tok_rows, top):
    picked = jnp.einsum("st,nsk->tnk", table, back, preferred_element_type=jnp.float32)
    return picked.reshape(tok_rows, top, -1)


def per_device(tokens, probs, routes, w_gate, w_up, w_down, cotangent):
    local_count = w_gate.shape[0]
    n_dp = lax.axis_size("dp")
    n_exp = lax.axis_size("expert")
    experts_all = local_count * n_exp
    tok_rows, width = tokens.shape
    top = routes.shape[1]
    capacity = max(2, 17 * tok_rows * top // (16 * experts_all))
    blocks = n_dp * n_exp
    slot_width = width // n_dp
    table = slot_table(routes, experts_all, capacity)
    x_send = spread_rows(table, jnp.repeat(tokens, top, axis=0), n_dp)
    x_send = x_send.reshape(blocks, local_count * capacity, slot_width)
    weight = probs.astype(jnp.float32)
    scaled = (jnp.repeat(cotangent, top, axis=0).astype(jnp.float32) * weight).astype(jnp.bfloat16)
    x_got = lax.all_to_all(x_send, ("dp", "expert"), split_axis=0, concat_axis=0, tiled=True)
    rows = to_rows(x_got, local_count)
    part = rows
    gate = jnp.einsum("red,edf->ref", part, w_gate, preferred_element_type=jnp.float32)
    upper = jnp.einsum("red,edf->ref", part, w_up, preferred_element_type=jnp.float32)
    summed = lax.psum_scatter(
        jnp.stack([gate, upper], axis=2).astype(jnp.bfloat16), "dp", scatter_dimension=0, tiled=True
    ).astype(jnp.float32)
    gate_pre = summed[:, :, 0]
    up_value = summed[:, :, 1]
    sig = jax.nn.sigmoid(gate_pre)
    act = (gate_pre * sig * up_value).astype(jnp.bfloat16)
    act_all = lax.all_gather(act, "dp", axis=0, tiled=True)
    result = jnp.einsum("ref,efd->red", act_all, w_down, preferred_element_type=jnp.float32).astype(
        jnp.bfloat16
    )
    outgoing = to_sources(result, capacity)
    back = lax.all_to_all(outgoing, ("dp", "expert"), split_axis=0, concat_axis=0, tiled=True)
    back = back.reshape(n_dp, experts_all * capacity, slot_width)
    picked = collect(table, back, tok_rows, top)
    mixed = jnp.sum(picked * weight[..., None], axis=1).astype(jnp.bfloat16)
    dy_send = spread_rows(table, scaled, n_dp).reshape(blocks, local_count * capacity, slot_width)
    dy_got = lax.all_to_all(dy_send, ("dp", "expert"), split_axis=0, concat_axis=0, tiled=True)
    dout = to_rows(dy_got, local_count)
    grad_down = jnp.einsum("ref,red->efd", act_all, dout, preferred_element_type=jnp.float32)
    part = dout
    dact = lax.psum_scatter(
        jnp.einsum("red,efd->ref", part, w_down, preferred_element_type=jnp.float32).astype(
            jnp.bfloat16
        ),
        "dp",
        scatter_dimension=0,
        tiled=True,
    ).astype(jnp.float32)
    dgate = (dact * up_value * sig * (1.0 + gate_pre * (1.0 - sig))).astype(jnp.bfloat16)
    dup = (dact * gate_pre * sig).astype(jnp.bfloat16)
    dgate_all, dup_all = (
        lax.all_gather(dgate, "dp", axis=0, tiled=True),
        lax.all_gather(dup, "dp", axis=0, tiled=True),
    )
    grad_gate = jnp.einsum("red,ref->edf", rows, dgate_all, preferred_element_type=jnp.float32)
    grad_up = jnp.einsum("red,ref->edf", rows, dup_all, preferred_element_type=jnp.float32)
    slot_grad = jnp.einsum(
        "ref,edf->red", dgate_all, w_gate, preferred_element_type=jnp.float32
    ) + jnp.einsum("ref,edf->red", dup_all, w_up, preferred_element_type=jnp.float32)
    slot_grad = slot_grad.astype(jnp.bfloat16)
    returned = lax.all_to_all(
        to_sources(slot_grad, capacity), ("dp", "expert"), split_axis=0, concat_axis=0, tiled=True
    )
    returned = returned.reshape(n_dp, experts_all * capacity, slot_width)
    input_grad = jnp.sum(collect(table, returned, tok_rows, top), axis=1).astype(jnp.bfloat16)
    return (
        mixed,
        input_grad,
        grad_gate.astype(jnp.bfloat16),
        grad_up.astype(jnp.bfloat16),
        grad_down.astype(jnp.bfloat16),
    )


def solution(mesh):
    return jax.shard_map(
        per_device,
        mesh=mesh,
        in_specs=(
            P(("dp", "expert"), None),
            P(("dp", "expert"), None),
            P(("dp", "expert"), None),
            P("expert", "dp", None),
            P("expert", "dp", None),
            P("expert", None, "dp"),
            P(("dp", "expert"), None),
        ),
        out_specs=(
            P(("dp", "expert"), None),
            P(("dp", "expert"), None),
            P("expert", "dp", None),
            P("expert", "dp", None),
            P("expert", None, "dp"),
        ),
        check_vma=False,
    )
```

profile of v0, /device:TPU:1, one launch (start us, length us, event | category | flops | bytes accessed | tf_op | source)
XLA Modules:
  0.0 326.0 jit_solution(5524149168156521085)
XLA Ops:
  7.2 0.8 fusion.55
  8.0 0.2 reduce_window_sum.11
  8.2 0.8 select_reduce_fusion
  9.1 0.7 multiply_add_fusion
  9.7 1.7 fusion.26
  11.4 0.3 reshape.232
  11.7 39.8 %all_to_all.20 = bf16[32,34,512]{2,1,0:T(8,128)(2,1)} all-to-all(bf16[32,34,512]{2,1,0:T(8,128)(2,1)S(1)} %reshape.232), channel_id=1, replica_groups=mesh['dp'=8,'expert'=4] {'dp','expert'}, dimensions={0} | all-to-all | bytes 2228224 | tf_op jit(solution)/shard_map/all_to_all | solution.py:58
  51.5 1.5 reshape.233
  53.0 1.3 fusion.1
  54.4 0.3 copy-done.8
  54.7 1.3 fusion.2
  56.0 0.4 pad_maximum_fusion
  56.4 9.6 %copy.22 = bf16[1088,1,2,1024]{3,2,1,0:T(2,128)(2,1)S(1)} copy(bf16[1088,1,2,1024]{3,0,2,1:T(8,128)(2,1)S(1)} %pad_maximum_fusion) | data formatting | bytes 8912896
  66.0 3.9 %copy.28 = bf16[136,8,2,1024]{3,1,2,0:T(8,128)(2,1)} copy(bf16[136,8,2,1024]{3,2,1,0:T(2,128)(2,1)S(1)} %bitcast.140) | data formatting | bytes 8912896
  69.9 0.6 copy-done.12
  70.5 0.6 copy-done.5
  71.1 0.3 multiply_convert_fusion
  71.4 0.4 fusion.27
  71.8 0.3 reshape.240
  72.2 35.4 %all_to_all.21 = bf16[32,34,512]{2,1,0:T(8,128)(2,1)} all-to-all(bf16[32,34,512]{2,1,0:T(8,128)(2,1)S(1)} %reshape.240), channel_id=1, replica_groups=mesh['dp'=8,'expert'=4] {'dp','expert'}, dimensions={0} | all-to-all | bytes 2228224 | tf_op jit(solution)/shard_map/all_to_all | solution.py:80
  107.6 1.5 reshape.241
  109.0 2.8 fusion.3
  111.9 11.7 %reduce-scatter.7.cloned.1.call-done = bf16[136,2048]{1,0:T(8,128)(2,1)} async-done(((bf16[1088,2048]{1,0:T(8,128)(2,1)}), bf16[136,2048]{1,0:T(8,128)(2,1)}) %reduce-scatter.7.cloned.1.call-update) | async-done | bytes 557072
  123.6 2.3 reshape.249
  125.9 0.1 copy_convert_fusion
  126.0 42.7 %reduce-scatter.5.cloned.1.call-done = bf16[136,1,1024]{2,0,1:T(8,128)(2,1)} async-done(((bf16[1088,1,1024]{2,0,1:T(8,128)(2,1)}), bf16[136,1,1024]{2,0,1:T(8,128)(2,1)}) %reduce-scatter.5.cloned.1.call-update) | async-done | bytes 278544 | tf_op jit(solution)/shard_map/reduce_scatter | solution.py:84
  168.8 2.2 fusion.51
  171.0 0.5 all-gather.8.cloned.1.call-update
  171.6 0.2 all-gather.4.cloned.1.call-start
  171.8 0.4 all-gather.4.cloned.1.call-update
  172.2 28.0 %all-gather.6.cloned.1.call-done = bf16[1088,1,1024]{2,0,1:T(8,128)(2,1)} async-done(((bf16[136,1,1024]{2,0,1:T(8,128)(2,1)}), bf16[1088,1,1024]{2,0,1:T(8,128)(2,1)}) %all-gather.6.cloned.1.call-update) | async-done | bytes 2228240 | tf_op jit(solution)/shard_map/all_gather | solution.py:95
  200.1 4.4 %fusion.12 = f32[1088,512]{1,0:T(8,128)} fusion(bf16[1088,1,1024]{2,0,1:T(8,128)(2,1)} %all-gather.6.cloned.1.call-done, bf16[1,512,1024]{2,1,0:T(8,128)(2,1)S(1)} %copy-done), kind=kOutput, calls=%fused_computation.20 | convolution fusion | flops 1140850688 | bytes 5505024 | tf_op jit(solution)/shard_map/ref,edf->red/dot_general | solution.py:100
  204.6 26.3 %all-gather.8.cloned.1.call-done = bf16[1088,1,1024]{2,0,1:T(8,128)(2,1)} async-done(((bf16[136,1,1024]{2,0,1:T(8,128)(2,1)}), bf16[1088,1,1024]{2,0,1:T(8,128)(2,1)}) %all-gather.8.cloned.1.call-update) | async-done | bytes 2228240 | tf_op jit(solution)/shard_map/all_gather | solution.py:96
  230.8 3.7 %fusion.6 = bf16[1088,1,512]{2,0,1:T(8,128)(2,1)S(1)} fusion(f32[1088,512]{1,0:T(8,128)} %fusion.12, bf16[1088,1,1024]{2,0,1:T(8,128)(2,1)} %all-gather.8.cloned.1.call-done, bf16[1,512,1024]{2,1,0:T(8,128)(2,1)S(1)} %copy-done.9), kind=kOutput, calls=%fused_computation.14 | convolution fusion | flops 1141964800 | bytes 6619136 | tf_op jit(solution)/shard_map/ref,edf->red/dot_general | solution.py:102
  234.5 1.3 reshape_transpose_reshape.9
  235.8 4.6 %all-to-all-start.3 = ((bf16[32,34,512]{2,1,0:T(8,128)(2,1)}), bf16[32,34,512]{2,1,0:T(8,128)(2,1)S(1)}, u32[]{:S(2)}, u32[]{:S(2)}) async-start(bf16[32,34,512]{2,1,0:T(8,128)(2,1)} %reshape_transpose_reshape.9), calls=%async_computation.4 | async-start | bytes 2621440 | tf_op jit(solution)/shard_map/all_to_all | solution.py:104
  240.5 33.1 %all-gather.4.cloned.1.call-done = bf16[1088,1,1024]{2,0,1:T(8,128)(2,1)} async-done(((bf16[136,1,1024]{2,0,1:T(8,128)(2,1)}), bf16[1088,1,1024]{2,0,1:T(8,128)(2,1)}) %all-gather.4.cloned.1.call-update) | async-done | bytes 2228240 | tf_op jit(solution)/shard_map/all_gather | solution.py:70
  273.6 4.0 %fusion.5 = bf16[1088,1,512]{2,0,1:T(8,128)(2,1)} fusion(bf16[1088,1,1024]{2,0,1:T(8,128)(2,1)} %all-gather.4.cloned.1.call-done, bf16[1,1024,512]{2,1,0:T(8,128)(2,1)S(1)} %copy-done.11), kind=kOutput, calls=%fused_computation.13 | convolution fusion | flops 1141407744 | bytes 4390912 | tf_op jit(solution)/shard_map/ref,efd->red/dot_general | solution.py:71
  277.6 2.4 reshape_transpose_reshape.8
  279.9 4.5 %all-to-all-start.1 = ((bf16[32,34,512]{2,1,0:T(8,128)(2,1)}), bf16[32,34,512]{2,1,0:T(8,128)(2,1)}, u32[]{:S(2)}, u32[]{:S(2)}) async-start(bf16[32,34,512]{2,1,0:T(8,128)(2,1)} %reshape_transpose_reshape.8), calls=%async_computation.1 | async-start | bytes 2621440 | tf_op jit(solution)/shard_map/all_to_all | solution.py:75
  284.5 4.3 %fusion.28 = bf16[1,512,1024]{2,1,0:T(8,128)(2,1)} fusion(bf16[1088,512]{1,0:T(8,128)(2,1)S(1)} %copy-done.2, bf16[1088,1,1024]{2,0,1:T(8,128)(2,1)} %all-gather.8.cloned.1.call-done), kind=kOutput, calls=%fused_computation.33 | convolution fusion | flops 1141374976 | bytes 4390912 | tf_op jit(solution)/shard_map/red,ref->edf/dot_general | solution.py:99
  288.8 2.5 fusion.31
  291.3 2.5 fusion.34
  293.9 0.3 reshape.244
  294.3 1.5 convolution_convert_fusion
  295.8 20.6 %all-to-all-done.1 = bf16[32,34,512]{2,1,0:T(8,128)(2,1)} async-done(((bf16[32,34,512]{2,1,0:T(8,128)(2,1)}), bf16[32,34,512]{2,1,0:T(8,128)(2,1)}, u32[]{:S(2)}, u32[]{:S(2)}) %all-to-all-start.1) | async-done | bytes 1114144 | tf_op jit(solution)/shard_map/all_to_all | solution.py:75
  316.4 1.5 reshape.238
  318.0 1.5 fusion
  (34 shorter events, 0.5 us)
Async XLA Ops:
  7.2 45.8 %copy-start = (bf16[1,512,1024]{2,1,0:T(8,128)(2,1)S(1)}, bf16[1,512,1024]{2,1,0:T(8,128)(2,1)}, u32[]{:S(2)}) copy-start(bf16[1,512,1024]{2,1,0:T(8,128)(2,1)} %param.10) | copy-start | bytes 3145732
  7.2 116.4 %reduce-scatter.7.cloned.1.call-start = ((), (), s32[]{:S(2)}) async-start(), calls=%async_computation.10 | async-start | bytes 5013504
  53.0 1.4 copy-start.1
  53.0 1.6 copy-start.8
  69.9 0.7 copy-start.12
  69.9 1.2 copy-start.5
  69.9 98.9 %reduce-scatter.5.cloned.1.call-start = ((), (), s32[]{:S(2)}) async-start(), calls=%async_computation.7 | async-start | bytes 2506752 | tf_op jit(solution)/shard_map/reduce_scatter | solution.py:84
  72.2 36.9 %copy-start.10 = (bf16[1,1024,512]{2,1,0:T(8,128)(2,1)S(1)}, bf16[1,1024,512]{2,1,0:T(8,128)(2,1)}, u32[]{:S(2)}) copy-start(bf16[1,1024,512]{2,1,0:T(8,128)(2,1)} %param.12) | copy-start | bytes 3145732
  109.0 2.8 copy-start.3
  111.8 88.3 %all-gather.6.cloned.1.call-start = ((), (), s32[]{:S(2)}) async-start(), calls=%async_computation.8 | async-start | bytes 2506752 | tf_op jit(solution)/shard_map/all_gather | solution.py:95
  171.0 59.8 %all-gather.8.cloned.1.call-start = ((), (), s32[]{:S(2)}) async-start(), calls=%async_computation.9 | async-start | bytes 2506752 | tf_op jit(solution)/shard_map/all_gather | solution.py:96
  171.6 102.0 %all-gather.4.cloned.1.call-start = ((), (), s32[]{:S(2)}) async-start(), calls=%async_computation.6 | async-start | bytes 2506752 | tf_op jit(solution)/shard_map/all_gather | solution.py:70
  172.1 58.7 %copy-start.9 = (bf16[1,512,1024]{2,1,0:T(8,128)(2,1)S(1)}, bf16[1,512,1024]{2,1,0:T(8,128)(2,1)}, u32[]{:S(2)}) copy-start(bf16[1,512,1024]{2,1,0:T(8,128)(2,1)} %param.11) | copy-start | bytes 3145732
  234.5 39.1 %copy-start.11 = (bf16[1,1024,512]{2,1,0:T(8,128)(2,1)S(1)}, bf16[1,1024,512]{2,1,0:T(8,128)(2,1)}, u32[]{:S(2)}) copy-start(bf16[1,1024,512]{2,1,0:T(8,128)(2,1)} %param.12) | copy-start | bytes 3145732
  235.8 44.1 %all-to-all-start.3 = ((bf16[32,34,512]{2,1,0:T(8,128)(2,1)}), bf16[32,34,512]{2,1,0:T(8,128)(2,1)S(1)}, u32[]{:S(2)}, u32[]{:S(2)}) async-start(bf16[32,34,512]{2,1,0:T(8,128)(2,1)} %reshape_transpose_reshape.9), calls=%async_computation.4 | async-start | bytes 2621440 | tf_op jit(solution)/shard_map/all_to_all | solution.py:104
  277.6 6.9 %copy-start.2 = (bf16[1088,512]{1,0:T(8,128)(2,1)S(1)}, bf16[1088,512]{1,0:T(8,128)(2,1)}, u32[]{:S(2)}) copy-start(bf16[1088,512]{1,0:T(8,128)(2,1)} %copy-done.1) | copy-start | bytes 3342340
  279.9 36.5 %all-to-all-start.1 = ((bf16[32,34,512]{2,1,0:T(8,128)(2,1)}), bf16[32,34,512]{2,1,0:T(8,128)(2,1)}, u32[]{:S(2)}, u32[]{:S(2)}) async-start(bf16[32,34,512]{2,1,0:T(8,128)(2,1)} %reshape_transpose_reshape.8), calls=%async_computation.1 | async-start | bytes 2621440 | tf_op jit(solution)/shard_map/all_to_all | solution.py:75
  284.5 4.3 %copy-start.6 = (bf16[1088,1,1024]{2,0,1:T(8,128)(2,1)S(1)}, bf16[1088,1,1024]{2,0,1:T(8,128)(2,1)}, u32[]{:S(2)}) copy-start(bf16[1088,1,1024]{2,0,1:T(8,128)(2,1)} %all-gather.6.cloned.1.call-done) | copy-start | bytes 6684676
  288.8 2.5 copy-start.4
  288.8 2.5 copy-start.7
Sparse Core Ops, SparseCore 0:
  70.0 53.5 reduce-scatter.6
  126.9 41.7 reduce-scatter.4
  171.2 28.8 all-gather.5
  202.5 28.3 all-gather.7
  233.1 40.3 all-gather.3
where the time goes:
time: 327 us; the launch traced here: 326 us
  waiting for transfers between devices  163 us (50%)
  blocking collectives  75.2 us (23%)
  matrix products  32 us (10%)
  local copies, waits for them, and re-layouts  26.5 us (8%)
  between operations  14.1 us (4%)
  starting transfers between devices  9.55 us (3%)
  other arithmetic  5.48 us (2%)
    reduce_scatter x1, waiting for transfers between devices, per_device(): lax.psum_scatter(jnp.einsum('red,efd->ref', part, w_down, preferred_eleme...  42.7 us
    all_to_all x1, blocking collectives, per_device(): lax.all_to_all(x_send, ('dp', 'expert'), split_axis=0, concat_axis=0, til...  39.8 us
    all_to_all x1, blocking collectives, per_device(): lax.all_to_all(dy_send, ('dp', 'expert'), split_axis=0, concat_axis=0, ti...  35.4 us
    all_gather x1, waiting for transfers between devices, per_device(): act_all = lax.all_gather(act, 'dp', axis=0, tiled=True)  33.1 us
    all_gather x1, waiting for transfers between devices, per_device(): lax.all_gather(dgate, 'dp', axis=0, tiled=True)  28 us
    all_gather x1, waiting for transfers between devices, per_device(): lax.all_gather(dup, 'dp', axis=0, tiled=True)  26.3 us
    all_to_all x1, waiting for transfers between devices, per_device(): lax.all_to_all(outgoing, ('dp', 'expert'), split_axis=0, concat_axis=0, t...  20.6 us
    unnamed x29, local copies, waits for them, and re-layouts  17.2 us
  transfers between devices with their start and end apart: 7, of which 6 were waited for; matrix products, arithmetic and copies ran while one was open for 11% of the time, Pallas kernels for 0%

commit v1 on v0

--- a/solution.py
+++ b/solution.py
@@ -67,7 +67,12 @@
     up_value = summed[:, :, 1]
     sig = jax.nn.sigmoid(gate_pre)
     act = (gate_pre * sig * up_value).astype(jnp.bfloat16)
-    act_all = lax.all_gather(act, "dp", axis=0, tiled=True)
+    ring = [act]
+    for hop in range(7):
+        ring.append(lax.ppermute(ring[-1], "dp", [(dev, (dev + 1) % 8) for dev in range(8)]))
+    act_all = jnp.roll(
+        jnp.concatenate(ring[::-1], axis=0), (lax.axis_index("dp") + 1) * ring[0].shape[0], axis=0
+    )
     result = jnp.einsum("ref,efd->red", act_all, w_down, preferred_element_type=jnp.float32).astype(
         jnp.bfloat16
     )

time: 327 us -> 312 us (0.954)
  waiting for transfers between devices: 163 us -> 126 us
  starting transfers between devices: 9.55 us -> 29.9 us
  local copies, waits for them, and re-layouts: 26.5 us -> 30.7 us
    all_gather x1 -> x0, waiting for transfers between devices: 33.1 us -> none  [per_device(): act_all = lax.all_gather(act, 'dp', axis=0, tiled=True)]
    ppermute x0 -> x7, waiting for transfers between devices: none -> 31.4 us  [per_device(): lax.ppermute(ring[-1], 'dp', [(dev, (dev + 1) % 8) for dev in range(8)])]
    all_gather x1, waiting for transfers between devices: 28 us -> 0.02 us  [per_device(): lax.all_gather(dgate, 'dp', axis=0, tiled=True)]
    all_to_all x1, waiting for transfers between devices: 0.01 us -> 18.1 us  [per_device(): lax.all_to_all(to_sources(slot_grad, capacity), ('dp', 'expert'), split_a...]
    ppermute x0 -> x7, starting transfers between devices: none -> 16.8 us  [per_device(): lax.ppermute(ring[-1], 'dp', [(dev, (dev + 1) % 8) for dev in range(8)])]
    all_to_all x1, waiting for transfers between devices: 20.6 us -> 5.69 us  [per_device(): lax.all_to_all(outgoing, ('dp', 'expert'), split_axis=0, concat_axis=0, t...]
    all_gather x1, waiting for transfers between devices: 26.3 us -> 16.6 us  [per_device(): lax.all_gather(dup, 'dp', axis=0, tiled=True)]
    all_to_all x1, starting transfers between devices: 4.54 us -> 9.75 us  [per_device(): lax.all_to_all(outgoing, ('dp', 'expert'), split_axis=0, concat_axis=0, t...]
  transfers between devices with their start and end apart: 7 -> 13, of which waited for: 6 -> 12; matrix products, arithmetic and copies ran while one was open for 11% -> 11% of each run, Pallas kernels for 0% -> 0%
where the time goes in v1:
time: 312 us
  waiting for transfers between devices  126 us (40%)
  blocking collectives  75.2 us (24%)
  local copies, waits for them, and re-layouts  30.7 us (10%)
  starting transfers between devices  29.9 us (10%)
  matrix products  29.9 us (10%)
  between operations  14.2 us (5%)
  other arithmetic  5.37 us (2%)
    reduce_scatter x1, waiting for transfers between devices, per_device(): lax.psum_scatter(jnp.einsum('red,efd->ref', part, w_down, preferred_eleme...  42.7 us
    all_to_all x1, blocking collectives, per_device(): lax.all_to_all(x_send, ('dp', 'expert'), split_axis=0, concat_axis=0, til...  39.8 us
    all_to_all x1, blocking collectives, per_device(): lax.all_to_all(dy_send, ('dp', 'expert'), split_axis=0, concat_axis=0, ti...  35.4 us
    ppermute x7, waiting for transfers between devices, per_device(): lax.ppermute(ring[-1], 'dp', [(dev, (dev + 1) % 8) for dev in range(8)])  31.4 us
    unnamed x44, local copies, waits for them, and re-layouts  19.5 us
    all_to_all x1, waiting for transfers between devices, per_device(): lax.all_to_all(to_sources(slot_grad, capacity), ('dp', 'expert'), split_a...  18.1 us
    ppermute x7, starting transfers between devices, per_device(): lax.ppermute(ring[-1], 'dp', [(dev, (dev + 1) % 8) for dev in range(8)])  16.8 us
    all_gather x1, waiting for transfers between devices, per_device(): lax.all_gather(dup, 'dp', axis=0, tiled=True)  16.6 us
  transfers between devices with their start and end apart: 13, of which 12 were waited for; matrix products, arithmetic and copies ran while one was open for 11% of the time, Pallas kernels for 0%

profile of v1, /device:TPU:1, one launch (start us, length us, event | category | flops | bytes accessed | tf_op | source)
XLA Modules:
  0.0 311.5 jit_solution(10330194249298606505)
XLA Ops:
  9.7 1.7 fusion.28
  11.8 39.8 %all_to_all.20 = bf16[32,34,512]{2,1,0:T(8,128)(2,1)} all-to-all(bf16[32,34,512]{2,1,0:T(8,128)(2,1)S(1)} %reshape.232), channel_id=1, replica_groups=mesh['dp'=8,'expert'=4] {'dp','expert'}, dimensions={0} | all-to-all | bytes 2228224 | tf_op jit(solution)/shard_map/all_to_all | solution.py:58
  51.6 1.5 reshape.233
  53.0 1.3 fusion.1
  54.7 1.3 fusion.2
  56.4 9.6 %copy.22 = bf16[1088,1,2,1024]{3,2,1,0:T(2,128)(2,1)S(1)} copy(bf16[1088,1,2,1024]{3,0,2,1:T(8,128)(2,1)S(1)} %pad_maximum_fusion) | data formatting | bytes 8912896
  66.0 3.9 %copy.28 = bf16[136,8,2,1024]{3,1,2,0:T(8,128)(2,1)} copy(bf16[136,8,2,1024]{3,2,1,0:T(2,128)(2,1)S(1)} %bitcast.140) | data formatting | bytes 8912896
  72.2 35.4 %all_to_all.21 = bf16[32,34,512]{2,1,0:T(8,128)(2,1)} all-to-all(bf16[32,34,512]{2,1,0:T(8,128)(2,1)S(1)} %reshape.240), channel_id=1, replica_groups=mesh['dp'=8,'expert'=4] {'dp','expert'}, dimensions={0} | all-to-all | bytes 2228224 | tf_op jit(solution)/shard_map/all_to_all | solution.py:85
  107.6 1.5 reshape.241
  109.1 2.8 fusion.3
  111.9 11.7 %reduce-scatter.7.cloned.1.call-done = bf16[136,2048]{1,0:T(8,128)(2,1)} async-done(((bf16[1088,2048]{1,0:T(8,128)(2,1)}), bf16[136,2048]{1,0:T(8,128)(2,1)}) %reduce-scatter.7.cloned.1.call-update) | async-done | bytes 557072
  123.6 2.3 reshape.249
  126.0 42.7 %reduce-scatter.5.cloned.1.call-done = bf16[136,1,1024]{2,0,1:T(8,128)(2,1)} async-done(((bf16[1088,1,1024]{2,0,1:T(8,128)(2,1)}), bf16[136,1,1024]{2,0,1:T(8,128)(2,1)}) %reduce-scatter.5.cloned.1.call-update) | async-done | bytes 278544 | tf_op jit(solution)/shard_map/reduce_scatter | solution.py:89
  168.8 2.1 fusion.53
  170.9 2.0 collective-permute-start
  172.9 3.5 %collective-permute-done = bf16[136,1,1024]{2,0,1:T(8,128)(2,1)S(1)} collective-permute-done((bf16[136,1,1024]{2,0,1:T(8,128)(2,1)S(1)}, bf16[136,1,1024]{2,0,1:T(8,128)(2,1)S(1)}, u32[]{:S(2)}, u32[]{:S(2)}) %collective-permute-start) | collective-permute-done | bytes 278560 | tf_op jit(solution)/shard_map/ppermute | solution.py:72
  176.4 2.5 collective-permute-start.1
  178.9 6.5 %collective-permute-done.1 = bf16[136,1,1024]{2,0,1:T(8,128)(2,1)S(1)} collective-permute-done((bf16[136,1,1024]{2,0,1:T(8,128)(2,1)S(1)}, bf16[136,1,1024]{2,0,1:T(8,128)(2,1)S(1)}, u32[]{:S(2)}, u32[]{:S(2)}) %collective-permute-start.1) | collective-permute-done | bytes 278560 | tf_op jit(solution)/shard_map/ppermute | solution.py:72
  185.4 2.5 collective-permute-start.2
  187.8 3.5 %collective-permute-done.2 = bf16[136,1,1024]{2,0,1:T(8,128)(2,1)S(1)} collective-permute-done((bf16[136,1,1024]{2,0,1:T(8,128)(2,1)S(1)}, bf16[136,1,1024]{2,0,1:T(8,128)(2,1)S(1)}, u32[]{:S(2)}, u32[]{:S(2)}) %collective-permute-start.2) | collective-permute-done | bytes 278560 | tf_op jit(solution)/shard_map/ppermute | solution.py:72
  191.3 2.5 collective-permute-start.3
  193.8 7.0 %collective-permute-done.3 = bf16[136,1,1024]{2,0,1:T(8,128)(2,1)S(1)} collective-permute-done((bf16[136,1,1024]{2,0,1:T(8,128)(2,1)S(1)}, bf16[136,1,1024]{2,0,1:T(8,128)(2,1)S(1)}, u32[]{:S(2)}, u32[]{:S(2)}) %collective-permute-start.3) | collective-permute-done | bytes 278560 | tf_op jit(solution)/shard_map/ppermute | solution.py:72
  200.8 2.5 collective-permute-start.4
  203.3 3.5 %collective-permute-done.4 = bf16[136,1,1024]{2,0,1:T(8,128)(2,1)S(1)} collective-permute-done((bf16[136,1,1024]{2,0,1:T(8,128)(2,1)S(1)}, bf16[136,1,1024]{2,0,1:T(8,128)(2,1)S(1)}, u32[]{:S(2)}, u32[]{:S(2)}) %collective-permute-start.4) | collective-permute-done | bytes 278560 | tf_op jit(solution)/shard_map/ppermute | solution.py:72
  206.8 2.5 collective-permute-start.5
  209.3 3.5 %collective-permute-done.5 = bf16[136,1,1024]{2,0,1:T(8,128)(2,1)S(1)} collective-permute-done((bf16[136,1,1024]{2,0,1:T(8,128)(2,1)S(1)}, bf16[136,1,1024]{2,0,1:T(8,128)(2,1)S(1)}, u32[]{:S(2)}, u32[]{:S(2)}) %collective-permute-start.5) | collective-permute-done | bytes 278560 | tf_op jit(solution)/shard_map/ppermute | solution.py:72
  212.8 2.5 collective-permute-start.6
  215.3 3.9 %collective-permute-done.6 = bf16[136,1,1024]{2,0,1:T(8,128)(2,1)S(1)} collective-permute-done((bf16[136,1,1024]{2,0,1:T(8,128)(2,1)S(1)}, bf16[136,1,1024]{2,0,1:T(8,128)(2,1)S(1)}, u32[]{:S(2)}, u32[]{:S(2)}) %collective-permute-start.6) | collective-permute-done | bytes 278560 | tf_op jit(solution)/shard_map/ppermute | solution.py:72
  219.6 2.0 copy-done.6
  221.7 1.3 fusion.5
  223.0 1.3 reshape_transpose_reshape.8
  224.3 9.8 %all-to-all-start.1 = ((bf16[32,34,512]{2,1,0:T(8,128)(2,1)}), bf16[32,34,512]{2,1,0:T(8,128)(2,1)S(1)}, u32[]{:S(2)}, u32[]{:S(2)}) async-start(bf16[32,34,512]{2,1,0:T(8,128)(2,1)} %reshape_transpose_reshape.8), calls=%async_computation.1 | async-start | bytes 2621440 | tf_op jit(solution)/shard_map/all_to_all | solution.py:80
  234.1 4.4 %fusion.12 = f32[1088,512]{1,0:T(8,128)} fusion(bf16[1088,1,1024]{2,0,1:T(8,128)(2,1)} %all-gather.3.cloned.1.call-done, bf16[1,512,1024]{2,1,0:T(8,128)(2,1)S(1)} %copy-done.10), kind=kOutput, calls=%fused_computation.20 | convolution fusion | flops 1140850688 | bytes 5505024 | tf_op jit(solution)/shard_map/ref,edf->red/dot_general | solution.py:105
  238.5 16.6 %all-gather.5.cloned.1.call-done = bf16[1088,1,1024]{2,0,1:T(8,128)(2,1)} async-done(((bf16[136,1,1024]{2,0,1:T(8,128)(2,1)}), bf16[1088,1,1024]{2,0,1:T(8,128)(2,1)}) %all-gather.5.cloned.1.call-update) | async-done | bytes 2228240 | tf_op jit(solution)/shard_map/all_gather | solution.py:101
  255.0 4.0 %fusion.6 = bf16[1088,1,512]{2,0,1:T(8,128)(2,1)S(1)} fusion(f32[1088,512]{1,0:T(8,128)} %fusion.12, bf16[1088,1,1024]{2,0,1:T(8,128)(2,1)} %all-gather.5.cloned.1.call-done, bf16[1,512,1024]{2,1,0:T(8,128)(2,1)} %param.11), kind=kOutput, calls=%fused_computation.14 | convolution fusion | flops 1141964800 | bytes 6619136 | tf_op jit(solution)/shard_map/ref,edf->red/dot_general | solution.py:107
  259.0 1.2 reshape_transpose_reshape.9
  260.2 5.7 %all-to-all-done.1 = bf16[32,34,512]{2,1,0:T(8,128)(2,1)S(1)} async-done(((bf16[32,34,512]{2,1,0:T(8,128)(2,1)}), bf16[32,34,512]{2,1,0:T(8,128)(2,1)S(1)}, u32[]{:S(2)}, u32[]{:S(2)}) %all-to-all-start.1) | async-done | bytes 1114144 | tf_op jit(solution)/shard_map/all_to_all | solution.py:80
  265.9 3.2 %all-to-all-start.3 = ((bf16[32,34,512]{2,1,0:T(8,128)(2,1)}), bf16[32,34,512]{2,1,0:T(8,128)(2,1)S(1)}, u32[]{:S(2)}, u32[]{:S(2)}) async-start(bf16[32,34,512]{2,1,0:T(8,128)(2,1)} %reshape_transpose_reshape.9), calls=%async_computation.4 | async-start | bytes 2621440 | tf_op jit(solution)/shard_map/all_to_all | solution.py:109
  269.1 4.6 %fusion.36 = bf16[1,1024,512]{2,1,0:T(8,128)(2,1)} fusion(bf16[1088,512]{1,0:T(8,128)(2,1)} %copy-done.4, bf16[2176,1,1024]{2,0,1:T(8,128)(2,1)} %copy-done.6, s32[]{:T(128)S(6)} %select_n.14), kind=kOutput, calls=%fused_computation.37 | convolution fusion | flops 1141374976 | bytes 4390916 | tf_op jit(solution)/shard_map/ref,red->efd/dot_general | solution.py:87
  273.7 2.5 fusion.30
  276.2 2.5 fusion.33
  278.7 1.2 reshape.238
  279.9 1.4 copy.26
  281.3 1.5 fusion
  282.8 18.1 %all-to-all-done.3 = bf16[32,34,512]{2,1,0:T(8,128)(2,1)S(1)} async-done(((bf16[32,34,512]{2,1,0:T(8,128)(2,1)}), bf16[32,34,512]{2,1,0:T(8,128)(2,1)S(1)}, u32[]{:S(2)}, u32[]{:S(2)}) %all-to-all-start.3) | async-done | bytes 1114144 | tf_op jit(solution)/shard_map/all_to_all | solution.py:109
  300.9 1.2 reshape.244
  302.1 1.4 copy.27
  303.5 1.5 convolution_convert_fusion
  (61 shorter events, 6.5 us)
Async XLA Ops:
  7.2 101.9 %copy-start = (bf16[1,1024,512]{2,1,0:T(8,128)(2,1)S(1)}, bf16[1,1024,512]{2,1,0:T(8,128)(2,1)}, u32[]{:S(2)}) copy-start(bf16[1,1024,512]{2,1,0:T(8,128)(2,1)} %param.12) | copy-start | bytes 3145732
  7.2 116.4 %reduce-scatter.7.cloned.1.call-start = ((), (), s32[]{:S(2)}) async-start(), calls=%async_computation.9 | async-start | bytes 5013504
  11.7 41.3 %copy-start.9 = (bf16[1,512,1024]{2,1,0:T(8,128)(2,1)S(1)}, bf16[1,512,1024]{2,1,0:T(8,128)(2,1)}, u32[]{:S(2)}) copy-start(bf16[1,512,1024]{2,1,0:T(8,128)(2,1)} %param.10) | copy-start | bytes 3145732
  53.0 1.4 copy-start.2
  53.0 1.6 copy-start.11
  69.9 0.7 copy-start.12
  69.9 1.2 copy-start.5
  69.9 98.9 %reduce-scatter.5.cloned.1.call-start = ((), (), s32[]{:S(2)}) async-start(), calls=%async_computation.6 | async-start | bytes 2506752 | tf_op jit(solution)/shard_map/reduce_scatter | solution.py:89
  109.0 2.8 copy-start.4
  111.8 122.2 %all-gather.3.cloned.1.call-start = ((), (), s32[]{:S(2)}) async-start(), calls=%async_computation.7 | async-start | bytes 2506752 | tf_op jit(solution)/shard_map/all_gather | solution.py:100
  170.9 84.1 %all-gather.5.cloned.1.call-start = ((), (), s32[]{:S(2)}) async-start(), calls=%async_computation.8 | async-start | bytes 2506752 | tf_op jit(solution)/shard_map/all_gather | solution.py:101
  170.9 5.5 %collective-permute-start = (bf16[136,1,1024]{2,0,1:T(8,128)(2,1)S(1)}, bf16[136,1,1024]{2,0,1:T(8,128)(2,1)S(1)}, u32[]{:S(2)}, u32[]{:S(2)}) collective-permute-start(bf16[136,1,1024]{2,0,1:T(8,128)(2,1)S(1)} %get-tuple-element.7), channel_id=1, source_target_pairs={{0,4},{4,8},{8,12},{12,16},{16,20},{20,24},{24,28},{28,0},{1,5},{5... | collective-permute-start | bytes 835592 | tf_op jit(solution)/shard_map/ppermute | solution.py:72
  176.4 9.0 %collective-permute-start.1 = (bf16[136,1,1024]{2,0,1:T(8,128)(2,1)S(1)}, bf16[136,1,1024]{2,0,1:T(8,128)(2,1)S(1)}, u32[]{:S(2)}, u32[]{:S(2)}) collective-permute-start(bf16[136,1,1024]{2,0,1:T(8,128)(2,1)S(1)} %collective-permute-done), channel_id=1, source_target_pairs={{0,4},{4,8},{8,12},{12,16},{16,20},{20,24},{24,28},{28,0},{1,5},{5... | collective-permute-start | bytes 835592 | tf_op jit(solution)/shard_map/ppermute | solution.py:72
  185.4 6.0 %collective-permute-start.2 = (bf16[136,1,1024]{2,0,1:T(8,128)(2,1)S(1)}, bf16[136,1,1024]{2,0,1:T(8,128)(2,1)S(1)}, u32[]{:S(2)}, u32[]{:S(2)}) collective-permute-start(bf16[136,1,1024]{2,0,1:T(8,128)(2,1)S(1)} %collective-permute-done.1), channel_id=1, source_target_pairs={{0,4},{4,8},{8,12},{12,16},{16,20},{20,24},{24,28},{28,0},{1,5},{5... | collective-permute-start | bytes 835592 | tf_op jit(solution)/shard_map/ppermute | solution.py:72
  191.3 9.5 %collective-permute-start.3 = (bf16[136,1,1024]{2,0,1:T(8,128)(2,1)S(1)}, bf16[136,1,1024]{2,0,1:T(8,128)(2,1)S(1)}, u32[]{:S(2)}, u32[]{:S(2)}) collective-permute-start(bf16[136,1,1024]{2,0,1:T(8,128)(2,1)S(1)} %collective-permute-done.2), channel_id=1, source_target_pairs={{0,4},{4,8},{8,12},{12,16},{16,20},{20,24},{24,28},{28,0},{1,5},{5... | collective-permute-start | bytes 835592 | tf_op jit(solution)/shard_map/ppermute | solution.py:72
  200.8 6.0 %collective-permute-start.4 = (bf16[136,1,1024]{2,0,1:T(8,128)(2,1)S(1)}, bf16[136,1,1024]{2,0,1:T(8,128)(2,1)S(1)}, u32[]{:S(2)}, u32[]{:S(2)}) collective-permute-start(bf16[136,1,1024]{2,0,1:T(8,128)(2,1)S(1)} %collective-permute-done.3), channel_id=1, source_target_pairs={{0,4},{4,8},{8,12},{12,16},{16,20},{20,24},{24,28},{28,0},{1,5},{5... | collective-permute-start | bytes 835592 | tf_op jit(solution)/shard_map/ppermute | solution.py:72
  206.8 6.0 %collective-permute-start.5 = (bf16[136,1,1024]{2,0,1:T(8,128)(2,1)S(1)}, bf16[136,1,1024]{2,0,1:T(8,128)(2,1)S(1)}, u32[]{:S(2)}, u32[]{:S(2)}) collective-permute-start(bf16[136,1,1024]{2,0,1:T(8,128)(2,1)S(1)} %collective-permute-done.4), channel_id=1, source_target_pairs={{0,4},{4,8},{8,12},{12,16},{16,20},{20,24},{24,28},{28,0},{1,5},{5... | collective-permute-start | bytes 835592 | tf_op jit(solution)/shard_map/ppermute | solution.py:72
  212.8 6.4 %collective-permute-start.6 = (bf16[136,1,1024]{2,0,1:T(8,128)(2,1)S(1)}, bf16[136,1,1024]{2,0,1:T(8,128)(2,1)S(1)}, u32[]{:S(2)}, u32[]{:S(2)}) collective-permute-start(bf16[136,1,1024]{2,0,1:T(8,128)(2,1)S(1)} %collective-permute-done.5), channel_id=1, source_target_pairs={{0,4},{4,8},{8,12},{12,16},{16,20},{20,24},{24,28},{28,0},{1,5},{5... | collective-permute-start | bytes 835592 | tf_op jit(solution)/shard_map/ppermute | solution.py:72
  219.6 2.1 copy-start.6
  223.0 11.1 %copy-start.10 = (bf16[1,512,1024]{2,1,0:T(8,128)(2,1)S(1)}, bf16[1,512,1024]{2,1,0:T(8,128)(2,1)}, u32[]{:S(2)}) copy-start(bf16[1,512,1024]{2,1,0:T(8,128)(2,1)} %param.10) | copy-start | bytes 3145732
  224.3 41.6 %all-to-all-start.1 = ((bf16[32,34,512]{2,1,0:T(8,128)(2,1)}), bf16[32,34,512]{2,1,0:T(8,128)(2,1)S(1)}, u32[]{:S(2)}, u32[]{:S(2)}) async-start(bf16[32,34,512]{2,1,0:T(8,128)(2,1)} %reshape_transpose_reshape.8), calls=%async_computation.1 | async-start | bytes 2621440 | tf_op jit(solution)/shard_map/all_to_all | solution.py:80
  265.9 35.0 %all-to-all-start.3 = ((bf16[32,34,512]{2,1,0:T(8,128)(2,1)}), bf16[32,34,512]{2,1,0:T(8,128)(2,1)S(1)}, u32[]{:S(2)}, u32[]{:S(2)}) async-start(bf16[32,34,512]{2,1,0:T(8,128)(2,1)} %reshape_transpose_reshape.9), calls=%async_computation.4 | async-start | bytes 2621440 | tf_op jit(solution)/shard_map/all_to_all | solution.py:109
  269.1 4.6 %copy-start.3 = (bf16[1088,512]{1,0:T(8,128)(2,1)S(1)}, bf16[1088,512]{1,0:T(8,128)(2,1)}, u32[]{:S(2)}) copy-start(bf16[1088,512]{1,0:T(8,128)(2,1)} %copy-done.2) | copy-start | bytes 3342340
  269.1 4.6 %copy-start.8 = (bf16[1088,1,1024]{2,0,1:T(8,128)(2,1)S(1)}, bf16[1088,1,1024]{2,0,1:T(8,128)(2,1)}, u32[]{:S(2)}) copy-start(bf16[1088,1,1024]{2,0,1:T(8,128)(2,1)} %all-gather.5.cloned.1.call-done) | copy-start | bytes 6684676
  273.7 2.5 copy-start.7
  300.9 4.1 %copy-start.1 = (bf16[1,1024,512]{2,1,0:T(8,128)(2,1)S(1)}, bf16[1,1024,512]{2,1,0:T(8,128)(2,1)}, u32[]{:S(2)}) copy-start(bf16[1,1024,512]{2,1,0:T(8,128)(2,1)} %param.12) | copy-start | bytes 3145732
Sparse Core Ops, SparseCore 0:
  70.0 53.5 reduce-scatter.6
  127.0 41.7 reduce-scatter.4
  171.3 32.4 all-gather.2
  215.4 39.5 all-gather.4
